TPU v7x, 256 devices: a whole 4x4x8 slice. The times are simulated.
256 devices in a mesh: alpha: 8 (over z_lo, y), beta: 32 (over z_hi, x, core).
Axes of the slice: x: 4, y: 4, z: 8 (z_hi: 4, z_lo: 2; z = z_hi * 2 + z_lo), core: 2. Of those that a mesh axis runs over, the one named last changes fastest.
Arguments:
- ci_vectors: bfloat16 [8, 4096, 4096], P(None, 'alpha', 'beta'), may hold values from -6 to 6
- alpha_blocks: bfloat16 [32, 16, 128, 128], P('alpha'), may hold values from -0.125 to 0.125
- alpha_cols: int32 [32, 16], P('alpha'), may hold values from 0 to 31, all different within a row
- beta_blocks: bfloat16 [32, 16, 128, 128], P('beta'), may hold values from -0.125 to 0.125
- beta_cols: int32 [32, 16], P('beta'), may hold values from 0 to 31, all different within a row
- diagonal: float32 [4096, 4096], P('alpha', 'beta'), may hold values from -1 to 3
Outputs:
- sigma_vectors: bfloat16 [8, 4096, 4096], P(None, 'alpha', 'beta')
Inputs may be any that keep to these rules, and one draw needn't show every extreme that they name: `alpha_cols`: each block-row names 16 different block-columns. `beta_cols`: each block-row names 16 different block-columns.
All inputs are finite; a program needn't handle non-finite values.
Results may differ from a plain program's by a relative error of at most 0.001.
Values may be sent and summed in bfloat16 or wider, within the bound.
A program may use at most 128 MiB of HBM per device.

v0:
```python
import jax
import jax.numpy as jnp
from jax import lax
from jax.sharding import PartitionSpec as P


def alpha_pass(ci_vectors, alpha_blocks, alpha_cols):
    vectors, rows_local, cols_local = ci_vectors.shape
    block = alpha_blocks.shape[-1]
    owned = alpha_blocks.shape[0]
    whole = lax.all_gather(ci_vectors, "alpha", axis=1, tiled=True)
    grid = whole.reshape(vectors, whole.shape[1] // block, block, cols_local)
    picked = grid[:, alpha_cols]
    term = jnp.einsum("rkij,vrkjb->vrib", alpha_blocks, picked, preferred_element_type=jnp.float32)
    return term.reshape(vectors, owned * block, cols_local)


def beta_pass(ci_vectors, beta_blocks, beta_cols):
    vectors, rows_local, cols_local = ci_vectors.shape
    block = beta_blocks.shape[-1]
    turned = lax.all_to_all(ci_vectors, "beta", split_axis=1, concat_axis=2, tiled=True)
    few_rows = turned.shape[1]
    all_cols = turned.shape[2]
    grid = turned.reshape(vectors, few_rows, all_cols // block, block)
    hb_piece = lax.all_gather(beta_blocks, "beta", axis=0, tiled=True)
    col_piece = lax.all_gather(beta_cols.astype(jnp.bfloat16), "beta", axis=0, tiled=True)
    columns = col_piece.astype(jnp.int32)
    count = hb_piece.shape[0]
    picked = grid[:, :, columns]
    term = jnp.einsum("vtnkj,nkij->vtni", picked, hb_piece, preferred_element_type=jnp.float32)
    updated = term.reshape(vectors, few_rows, count * block)
    return lax.all_to_all(updated, "beta", split_axis=2, concat_axis=1, tiled=True)


def shards(ci_vectors, alpha_blocks, alpha_cols, beta_blocks, beta_cols, diagonal):
    alpha_part = alpha_pass(ci_vectors, alpha_blocks, alpha_cols)
    beta_part = beta_pass(ci_vectors, beta_blocks, beta_cols)
    total = alpha_part + beta_part + diagonal[None, :, :] * ci_vectors.astype(jnp.float32)
    return total.astype(jnp.bfloat16)


def solution(mesh):
    placed = (
        P(None, "alpha", "beta"),
        P("alpha", None, None, None),
        P("alpha", None),
        P("beta", None, None, None),
        P("beta", None),
        P("alpha", "beta"),
    )
    return jax.shard_map(
        shards, mesh=mesh, in_specs=placed, out_specs=P(None, "alpha", "beta"), check_vma=False
    )
```

profile of v0, /device:TPU:1, one launch (start us, length us, event | category | flops | bytes accessed | tf_op | source)
XLA Modules:
  0.0 348.9 jit_solution(12847920623883171120)
XLA Ops:
  6.5 0.0 copy-start
  6.5 0.0 all-gather.6.cloned.1.call-start
  6.5 0.7 all-gather.6.cloned.1.call-update
  7.3 0.0 all-gather.4.cloned.1.call-start
  7.3 0.7 all-gather.4.cloned.1.call-update
  8.0 2.9 copy.22
  10.9 12.6 %all-to-all-start = ((bf16[8,512,128]{2,0,1:T(8,128)(2,1)}), bf16[8,512,128]{2,0,1:T(8,128)(2,1)}, u32[]{:S(2)}, u32[]{:S(2)}) async-start(bf16[8,512,128]{2,0,1:T(8,128)(2,1)} %copy.22), calls=%async_computation | async-start | bytes 2097152 | tf_op jit(solution)/shard_map/all_to_all | solution.py:21
  23.5 0.7 convert_bitcast_fusion
  24.2 72.8 %all-gather = bf16[32,1,16]{2,1,0:T(2,128)(2,1)S(1)} all-gather(bf16[1,1,16]{2,1,0:T(2,128)(2,1)S(1)} %convert_bitcast_fusion), channel_id=1, replica_groups=mesh['alpha'=8,'beta'=32] {'beta'}, dimensions={0}, use_global_device_ids=true | all-gather | bytes 1056 | tf_op jit(solution)/shard_map/all_gather | solution.py:26
  97.0 0.1 reshape.25
  97.1 0.0 all-to-all-done
  97.1 1.4 copy.23
  98.4 15.0 %gather_fusion.1 = bf16[512,8,16,128]{3,2,1,0:T(8,128)(2,1)} fusion(bf16[8,16,32,128]{3,1,2,0:T(8,128)(2,1)S(1)} %bitcast.62, s32[1024]{0:T(1024)S(1)} %pad_clamp_fusion), kind=kCustom, calls=%fused_computation.1 | custom fusion | bytes 33556480 | tf_op jit(solution)/shard_map/gather | solution.py:29
  113.4 24.0 %all-gather.6.cloned.1.call-done = bf16[32,16,128,128]{3,2,1,0:T(8,128)(2,1)} async-done(((bf16[1,16,128,128]{3,2,1,0:T(8,128)(2,1)}), bf16[32,16,128,128]{3,2,1,0:T(8,128)(2,1)}) %all-gather.6.cloned.1.call-update) | async-done | bytes 16777232 | tf_op jit(solution)/shard_map/all_gather | solution.py:25
  137.3 14.3 %fusion.9 = f32[8,16,32,128]{3,1,0,2:T(8,128)} fusion(bf16[8,16,32,16,128]{4,1,0,3,2:T(8,128)(2,1)} %bitcast.66, bf16[32,16,128,128]{3,2,1,0:T(8,128)(2,1)} %all-gather.6.cloned.1.call-done), kind=kOutput, calls=%fused_computation.10 | convolution fusion | flops 2147483648 | bytes 35651584 | tf_op jit(solution)/shard_map/vtnkj,nkij->vtni/dot_general | solution.py:30
  151.6 9.5 %copy.33 = f32[8,16,32,128]{1,0,3,2:T(8,128)} copy(f32[8,16,32,128]{3,1,0,2:T(8,128)} %fusion.9) | data formatting | bytes 4194304 | tf_op jit(solution)/shard_map/reshape | solution.py:31
  161.1 0.0 copy-start.3
  161.1 13.2 %reshape.42 = f32[32,1,16384]{2,1,0:T(1,128)} reshape(f32[4096,8,16]{2,1,0:T(8,128)} %bitcast.64) | data formatting | bytes 4194304
  174.3 20.3 %all-to-all-start.1 = ((f32[32,1,16384]{2,1,0:T(1,128)}), f32[32,1,16384]{2,1,0:T(1,128)}, u32[]{:S(2)}, u32[]{:S(2)}) async-start(f32[32,1,16384]{2,1,0:T(1,128)} %reshape.42), calls=%async_computation.1 | async-start | bytes 4194304 | tf_op jit(solution)/shard_map/all_to_all | solution.py:32
  194.6 0.0 copy-done.3
  194.7 0.1 reshape.17
  194.8 95.1 %all-gather.4.cloned.1.call-done = bf16[8,4096,128]{2,1,0:T(8,128)(2,1)} async-done(((bf16[8,512,128]{2,1,0:T(8,128)(2,1)}), bf16[8,4096,128]{2,1,0:T(8,128)(2,1)}) %all-gather.4.cloned.1.call-update) | async-done | bytes 8388624 | tf_op jit(solution)/shard_map/all_gather | solution.py:11
  289.9 11.0 %gather_fusion = bf16[64,8,128,128]{3,2,1,0:T(8,128)(2,1)} fusion(bf16[8,32,128,128]{3,2,1,0:T(8,128)(2,1)} %bitcast.67, s32[1024]{0:T(1024)S(1)} %pad_clamp_fusion.1), kind=kCustom, calls=%fused_computation | custom fusion | bytes 33554688 | tf_op jit(solution)/shard_map/gather | solution.py:13
  300.9 0.0 copy-done
  300.9 7.1 %fusion.6 = f32[8,4,128,128]{3,2,0,1:T(8,128)S(1)} fusion(bf16[8,4,16,128,128]{4,3,0,2,1:T(8,128)(2,1)} %bitcast.63, bf16[4,16,128,128]{3,2,1,0:T(8,128)(2,1)S(1)} %copy-done), kind=kOutput, calls=%fused_computation.9 | convolution fusion | flops 2147483648 | bytes 20971520 | tf_op jit(solution)/shard_map/rkij,vrkjb->vrib/dot_general | solution.py:14
  308.0 1.5 copy.21
  309.4 0.0 all-to-all-done.1
  309.4 0.5 broadcast.9
  309.9 8.7 %reduce = f32[32,16384]{1,0:T(8,128)} reduce(f32[32,1,16384]{2,1,0:T(1,128)} %all-to-all-done.1, f32[]{:T(128)} %broadcast.9), dimensions={1}, to_apply=%all_to_all.27.reduce_sub_computation | reduce | bytes 4194308 | tf_op jit(solution)/shard_map/all_to_all | solution.py:32
  318.7 9.2 %reshape.43 = f32[4096,8,16]{2,1,0:T(8,128)} reshape(f32[32,16384]{1,0:T(8,128)} %reduce) | data formatting | bytes 4194304
  327.8 0.0 copy-start.1
  327.8 0.0 copy-start.2
  327.8 10.7 %copy.28 = f32[8,32,16,128]{3,2,1,0:T(8,128)} copy(f32[8,32,16,128]{2,0,3,1:T(8,128)} %bitcast.65) | data formatting | bytes 4194304 | tf_op jit(solution)/shard_map/all_to_all | solution.py:32
  338.5 0.0 copy-done.1
  338.5 0.0 copy-done.2
  338.5 3.5 %fusion.5 = bf16[8,512,128]{2,1,0:T(8,128)(2,1)} fusion(f32[8,32,16,128]{3,2,1,0:T(8,128)} %copy.28, f32[8,4,128,128]{3,2,1,0:T(8,128)} %copy.21, bf16[8,512,128]{2,1,0:T(8,128)(2,1)S(1)} %copy-done.1, f32[512,128]{1,0:T(8,128)S(1)} %copy-done.2), kind=kLoop, calls=%fused_computation.8 | loop fusion | flops 2621440 | bytes 6553600 | tf_op jit(solution)/shard_map/convert_element_type | solution.py:39
  (5 shorter events, 0.0 us)
Async XLA Ops:
  6.5 294.4 %copy-start = (bf16[4,16,128,128]{3,2,1,0:T(8,128)(2,1)S(1)}, bf16[4,16,128,128]{3,2,1,0:T(8,128)(2,1)}, u32[]{:S(2)}) copy-start(bf16[4,16,128,128]{3,2,1,0:T(8,128)(2,1)} %param.7) | copy-start | bytes 6291460
  6.5 130.8 %all-gather.6.cloned.1.call-start = ((), (), s32[]{:S(2)}) async-start(), calls=%async_computation.3 | async-start | bytes 17301504 | tf_op jit(solution)/shard_map/all_gather | solution.py:25
  7.3 282.6 %all-gather.4.cloned.1.call-start = ((), (), s32[]{:S(2)}) async-start(), calls=%async_computation.2 | async-start | bytes 9437184 | tf_op jit(solution)/shard_map/all_gather | solution.py:11
  10.9 86.2 %all-to-all-start = ((bf16[8,512,128]{2,0,1:T(8,128)(2,1)}), bf16[8,512,128]{2,0,1:T(8,128)(2,1)}, u32[]{:S(2)}, u32[]{:S(2)}) async-start(bf16[8,512,128]{2,0,1:T(8,128)(2,1)} %copy.22), calls=%async_computation | async-start | bytes 2097152 | tf_op jit(solution)/shard_map/all_to_all | solution.py:21
  161.1 33.5 %copy-start.3 = (s32[4,16]{1,0:T(4,128)S(1)}, s32[4,16]{1,0:T(4,128)}, u32[]{:S(2)}) copy-start(s32[4,16]{1,0:T(4,128)} %param.8) | copy-start | bytes 772
  174.3 135.1 %all-to-all-start.1 = ((f32[32,1,16384]{2,1,0:T(1,128)}), f32[32,1,16384]{2,1,0:T(1,128)}, u32[]{:S(2)}, u32[]{:S(2)}) async-start(f32[32,1,16384]{2,1,0:T(1,128)} %reshape.42), calls=%async_computation.1 | async-start | bytes 4194304 | tf_op jit(solution)/shard_map/all_to_all | solution.py:32
  327.8 10.7 %copy-start.1 = (bf16[8,512,128]{2,1,0:T(8,128)(2,1)S(1)}, bf16[8,512,128]{2,1,0:T(8,128)(2,1)}, u32[]{:S(2)}) copy-start(bf16[8,512,128]{2,1,0:T(8,128)(2,1)} %param.6) | copy-start | bytes 3145732
  327.8 10.7 %copy-start.2 = (f32[512,128]{1,0:T(8,128)S(1)}, f32[512,128]{1,0:T(8,128)}, u32[]{:S(2)}) copy-start(f32[512,128]{1,0:T(8,128)} %param.11) | copy-start | bytes 786436
Sparse Core Ops, SparseCore 0:
  9.9 127.4 all-gather.5
  139.1 150.6 all-gather.3
where the time goes:
time: 350 us; the launch traced here: 349 us
  waiting for transfers between devices  120 us (34%)
  local copies, waits for them, and re-layouts  74.9 us (21%)
  blocking collectives  72.8 us (21%)
  starting transfers between devices  33 us (9%)
  matrix products  21.3 us (6%)
  between operations  13.5 us (4%)
  other arithmetic  13 us (4%)
    all_gather x1, waiting for transfers between devices, alpha_pass(): whole = lax.all_gather(ci_vectors, 'alpha', axis=1, tiled=True)  95.1 us
    all_gather x1, blocking collectives, beta_pass(): lax.all_gather(beta_cols.astype(jnp.bfloat16), 'beta', axis=0, tiled=True)  72.8 us
    unnamed x11, local copies, waits for them, and re-layouts  25.2 us
    all_gather x1, waiting for transfers between devices, beta_pass(): hb_piece = lax.all_gather(beta_blocks, 'beta', axis=0, tiled=True)  24 us
    all_to_all x1, starting transfers between devices, beta_pass(): lax.all_to_all(updated, 'beta', split_axis=2, concat_axis=1, tiled=True)  20.3 us
    gather x1, local copies, waits for them, and re-layouts, beta_pass(): picked = grid[:, :, columns]  15 us
    dot_general x1, matrix products, beta_pass(): jnp.einsum('vtnkj,nkij->vtni', picked, hb_piece, preferred_element_type=j...  14.3 us
    all_to_all x1, starting transfers between devices, beta_pass(): lax.all_to_all(ci_vectors, 'beta', split_axis=1, concat_axis=2, tiled=True)  12.6 us
  transfers between devices with their start and end apart: 4, of which 2 were waited for; matrix products, arithmetic and copies ran while one was open for 22% of the time, Pallas kernels for 0%

commit v1 on v0

--- a/solution.py
+++ b/solution.py
@@ -22,7 +22,9 @@
     few_rows = turned.shape[1]
     all_cols = turned.shape[2]
     grid = turned.reshape(vectors, few_rows, all_cols // block, block)
-    hb_piece = lax.all_gather(beta_blocks, "beta", axis=0, tiled=True)
+    hb_piece = jnp.concatenate(
+        lax.all_to_all(jnp.stack([beta_blocks] * lax.axis_size("beta")), "beta", 0, 0), axis=0
+    )
     col_piece = lax.all_gather(beta_cols.astype(jnp.bfloat16), "beta", axis=0, tiled=True)
     columns = col_piece.astype(jnp.int32)
     count = hb_piece.shape[0]

time: 350 us -> 688 us (1.97); the launches traced: 349 us -> 676 us
  blocking collectives: 72.8 us -> 516 us
  waiting for transfers between devices: 120 us -> 20.6 us
  starting transfers between devices: 33 us -> 11.6 us
    all_gather x1, blocking collectives: 72.8 us -> 476 us  [beta_pass(): lax.all_gather(beta_cols.astype(jnp.bfloat16), 'beta', axis=0, tiled=True)]
    all_gather x1, waiting for transfers between devices: 95.1 us -> 0.01 us  [alpha_pass(): whole = lax.all_gather(ci_vectors, 'alpha', axis=1, tiled=True)]
    all_to_all x0 -> x1, blocking collectives: none -> 40.1 us  [beta_pass(): lax.all_to_all(ci_vectors, 'beta', split_axis=1, concat_axis=2, tiled=True)]
    all_gather x1 -> x0, waiting for transfers between devices: 24 us -> none  [beta_pass(): hb_piece = lax.all_gather(beta_blocks, 'beta', axis=0, tiled=True)]
    all_to_all x1, waiting for transfers between devices: 0.01 us -> 19.9 us  [beta_pass(): lax.all_to_all(updated, 'beta', split_axis=2, concat_axis=1, tiled=True)]
    all_to_all x1, starting transfers between devices: 20.3 us -> 4.9 us  [beta_pass(): lax.all_to_all(updated, 'beta', split_axis=2, concat_axis=1, tiled=True)]
    another operation x0 -> x1, local copies, waits for them, and re-layouts: none -> 7.01 us  [beta_pass(): jnp.stack([beta_blocks] * lax.axis_size('beta'))]
    unnamed x11 -> x13, local copies, waits for them, and re-layouts: 25.2 us -> 24.3 us
  transfers between devices with their start and end apart: 4 -> 3, of which waited for: 2 -> 1; matrix products, arithmetic and copies ran while one was open for 22% -> 11% of each run, Pallas kernels for 0% -> 0%
where the time goes in v1:
time: 688 us; the launch traced here: 676 us
  blocking collectives  516 us (75%)
  local copies, waits for them, and re-layouts  81 us (12%)
  matrix products  21.3 us (3%)
  waiting for transfers between devices  20.6 us (3%)
  between operations  13.5 us (2%)
  other arithmetic  12.3 us (2%)
  starting transfers between devices  11.6 us (2%)
    all_gather x1, blocking collectives, beta_pass(): lax.all_gather(beta_cols.astype(jnp.bfloat16), 'beta', axis=0, tiled=True)  476 us
    all_to_all x1, blocking collectives, beta_pass(): lax.all_to_all(ci_vectors, 'beta', split_axis=1, concat_axis=2, tiled=True)  40.1 us
    unnamed x13, local copies, waits for them, and re-layouts  24.3 us
    all_to_all x1, waiting for transfers between devices, beta_pass(): lax.all_to_all(updated, 'beta', split_axis=2, concat_axis=1, tiled=True)  19.9 us
    gather x1, local copies, waits for them, and re-layouts, beta_pass(): picked = grid[:, :, columns]  15 us
    dot_general x1, matrix products, beta_pass(): jnp.einsum('vtnkj,nkij->vtni', picked, hb_piece, preferred_element_type=j...  14.2 us
  transfers between devices with their start and end apart: 3, of which 1 were waited for; matrix products, arithmetic and copies ran while one was open for 11% of the time, Pallas kernels for 0%

profile of v1, /device:TPU:1, one launch (start us, length us, event | category | flops | bytes accessed | tf_op | source)
XLA Modules:
  0.0 676.0 jit_solution(7027852549541332283)
XLA Ops:
  6.5 0.0 copy-start
  6.5 2.1 copy.22
  8.6 40.1 %all_to_all.38 = bf16[8,512,128]{2,0,1:T(8,128)(2,1)} all-to-all(bf16[8,512,128]{2,0,1:T(8,128)(2,1)S(1)} %copy.22), channel_id=1, replica_groups=mesh['alpha'=8,'beta'=32] {'beta'}, dimensions={1} | all-to-all | bytes 2097152 | tf_op jit(solution)/shard_map/all_to_all | solution.py:21
  48.7 7.0 %stack.2 = bf16[32,1,16,128,128]{4,3,2,1,0:T(8,128)(2,1)} broadcast(bf16[16,128,128]{2,1,0:T(8,128)(2,1)} %bitcast.70), dimensions={2,3,4} | broadcast | bytes 17301504 | tf_op jit(solution)/shard_map/stack | solution.py:26
  55.7 0.0 copy-start.4
  55.7 6.7 all-to-all-start.1
  62.4 0.0 all-gather.3.cloned.1.call-start
  62.4 0.7 all-gather.3.cloned.1.call-update
  63.1 0.0 copy-done.4
  63.1 475.6 %all-gather = bf16[32,1,16]{2,1,0:T(2,128)(2,1)S(1)} all-gather(bf16[1,1,16]{2,1,0:T(2,128)(2,1)S(1)} %convert_bitcast_fusion), channel_id=1, replica_groups=mesh['alpha'=8,'beta'=32] {'beta'}, dimensions={0}, use_global_device_ids=true | all-gather | bytes 1056 | tf_op jit(solution)/shard_map/all_gather | solution.py:28
  538.8 0.1 reshape.32
  538.9 1.4 copy.23
  540.3 15.0 %gather_fusion.1 = bf16[512,8,16,128]{3,2,1,0:T(8,128)(2,1)} fusion(bf16[8,16,32,128]{3,1,2,0:T(8,128)(2,1)S(1)} %bitcast.64, s32[1024]{0:T(1024)S(1)} %pad_clamp_fusion), kind=kCustom, calls=%fused_computation.1 | custom fusion | bytes 33556480 | tf_op jit(solution)/shard_map/gather | solution.py:31
  555.2 0.0 all-to-all-done.1
  555.2 14.2 %fusion.9 = f32[8,16,32,128]{3,1,0,2:T(8,128)} fusion(bf16[8,16,32,16,128]{4,1,0,3,2:T(8,128)(2,1)} %bitcast.68, bf16[32,1,16,128,128]{4,3,2,1,0:T(8,128)(2,1)} %all-to-all-done.1), kind=kOutput, calls=%fused_computation.10 | convolution fusion | flops 2147483648 | bytes 35651584 | tf_op jit(solution)/shard_map/vtnkj,nkij->vtni/dot_general | solution.py:32
  569.5 9.5 %copy.33 = f32[8,16,32,128]{1,0,3,2:T(8,128)} copy(f32[8,16,32,128]{3,1,0,2:T(8,128)} %fusion.9) | data formatting | bytes 4194304 | tf_op jit(solution)/shard_map/reshape | solution.py:33
  579.0 0.0 copy-start.3
  579.0 13.0 %reshape.49 = f32[32,1,16384]{2,1,0:T(1,128)} reshape(f32[4096,8,16]{2,1,0:T(8,128)} %bitcast.66) | data formatting | bytes 4194304
  592.0 4.9 all-to-all-start.2
  596.9 0.0 copy-done.3
  596.9 0.1 reshape.24
  597.0 0.0 all-gather.3.cloned.1.call-done
  597.0 11.0 %gather_fusion = bf16[64,8,128,128]{3,2,1,0:T(8,128)(2,1)} fusion(bf16[8,32,128,128]{3,2,1,0:T(8,128)(2,1)} %bitcast.69, s32[1024]{0:T(1024)S(1)} %pad_clamp_fusion.1), kind=kCustom, calls=%fused_computation | custom fusion | bytes 33554688 | tf_op jit(solution)/shard_map/gather | solution.py:13
  608.0 0.0 copy-done
  608.0 7.0 %fusion.6 = f32[8,4,128,128]{3,2,0,1:T(8,128)S(1)} fusion(bf16[8,4,16,128,128]{4,3,0,2,1:T(8,128)(2,1)} %bitcast.65, bf16[4,16,128,128]{3,2,1,0:T(8,128)(2,1)S(1)} %copy-done), kind=kOutput, calls=%fused_computation.9 | convolution fusion | flops 2147483648 | bytes 20971520 | tf_op jit(solution)/shard_map/rkij,vrkjb->vrib/dot_general | solution.py:14
  615.1 1.5 copy.21
  616.6 19.9 %all-to-all-done.2 = f32[32,1,16384]{2,1,0:T(1,128)} async-done(((f32[32,1,16384]{2,1,0:T(1,128)}), f32[32,1,16384]{2,1,0:T(1,128)}, u32[]{:S(2)}, u32[]{:S(2)}) %all-to-all-start.2) | async-done | bytes 2097184 | tf_op jit(solution)/shard_map/all_to_all | solution.py:34
  636.5 0.5 broadcast.12
  637.0 8.7 %reduce = f32[32,16384]{1,0:T(8,128)} reduce(f32[32,1,16384]{2,1,0:T(1,128)} %all-to-all-done.2, f32[]{:T(128)} %broadcast.12), dimensions={1}, to_apply=%all_to_all.31.reduce_sub_computation | reduce | bytes 4194308 | tf_op jit(solution)/shard_map/all_to_all | solution.py:34
  645.7 9.2 %reshape.50 = f32[4096,8,16]{2,1,0:T(8,128)} reshape(f32[32,16384]{1,0:T(8,128)} %reduce) | data formatting | bytes 4194304
  654.9 0.0 copy-start.1
  654.9 0.0 copy-start.2
  654.9 10.7 %copy.28 = f32[8,32,16,128]{3,2,1,0:T(8,128)} copy(f32[8,32,16,128]{2,0,3,1:T(8,128)} %bitcast.67) | data formatting | bytes 4194304 | tf_op jit(solution)/shard_map/all_to_all | solution.py:34
  665.6 0.0 copy-done.1
  665.6 0.0 copy-done.2
  665.6 3.5 fusion.5
  (6 shorter events, 0.0 us)
Async XLA Ops:
  6.5 601.5 %copy-start = (bf16[4,16,128,128]{3,2,1,0:T(8,128)(2,1)S(1)}, bf16[4,16,128,128]{3,2,1,0:T(8,128)(2,1)}, u32[]{:S(2)}) copy-start(bf16[4,16,128,128]{3,2,1,0:T(8,128)(2,1)} %param.7) | copy-start | bytes 6291460
  55.7 7.4 %copy-start.4 = (s32[1,16]{1,0:T(1,128)S(1)}, s32[1,16]{1,0:T(1,128)}, u32[]{:S(2)}) copy-start(s32[1,16]{1,0:T(1,128)} %param.10) | copy-start | bytes 196
  55.7 499.5 %all-to-all-start.1 = ((bf16[32,1,16,128,128]{4,3,2,1,0:T(8,128)(2,1)}), bf16[32,1,16,128,128]{4,3,2,1,0:T(8,128)(2,1)}, u32[]{:S(2)}, u32[]{:S(2)}) async-start(bf16[32,1,16,128,128]{4,3,2,1,0:T(8,128)(2,1)} %stack.2), calls=%async_computation.1 | async-start | bytes 33554432 | tf_op jit(solution)/shard_map/all_to_all | solution.py:26
  62.4 534.6 %all-gather.3.cloned.1.call-start = ((), (), s32[]{:S(2)}) async-start(), calls=%async_computation.3 | async-start | bytes 9437184 | tf_op jit(solution)/shard_map/all_gather | solution.py:11
  579.0 17.9 %copy-start.3 = (s32[4,16]{1,0:T(4,128)S(1)}, s32[4,16]{1,0:T(4,128)}, u32[]{:S(2)}) copy-start(s32[4,16]{1,0:T(4,128)} %param.8) | copy-start | bytes 772
  592.0 44.5 %all-to-all-start.2 = ((f32[32,1,16384]{2,1,0:T(1,128)}), f32[32,1,16384]{2,1,0:T(1,128)}, u32[]{:S(2)}, u32[]{:S(2)}) async-start(f32[32,1,16384]{2,1,0:T(1,128)} %reshape.49), calls=%async_computation.2 | async-start | bytes 4194304 | tf_op jit(solution)/shard_map/all_to_all | solution.py:34
  654.9 10.7 %copy-start.1 = (bf16[8,512,128]{2,1,0:T(8,128)(2,1)S(1)}, bf16[8,512,128]{2,1,0:T(8,128)(2,1)}, u32[]{:S(2)}) copy-start(bf16[8,512,128]{2,1,0:T(8,128)(2,1)} %param.6) | copy-start | bytes 3145732
  654.9 10.7 %copy-start.2 = (f32[512,128]{1,0:T(8,128)S(1)}, f32[512,128]{1,0:T(8,128)}, u32[]{:S(2)}) copy-start(f32[512,128]{1,0:T(8,128)} %param.11) | copy-start | bytes 786436
Sparse Core Ops, SparseCore 0:
  65.0 298.8 all-gather.2
